TPU v7x, 32 devices: a whole 2x2x4 slice. The times are simulated.
32 devices in a mesh: freq: 16 (over z, y, x), plane: 2 (over core).
Axes of the slice: x: 2, y: 2, z: 4, core: 2. Of those that a mesh axis runs over, the one named last changes fastest.
Arguments:
- state_in: float32 [2, 32, 5, 256, 128], P(None, 'freq', None, 'plane'), may hold values from -6 to 6
- forcing_in: float32 [2, 32, 5, 256, 128], P(None, 'freq', None, 'plane'), may hold values from -6 to 6
- base_flow: float32 [16, 5, 256, 128], P('freq', None, 'plane'), may hold values from -1 to 1
- station_index: int32 [2], replicated, may hold values from 0 to 15
- lobe_count: int32 [1], replicated, may hold values from 3 to 127
Outputs:
- state_out: float32 [2, 32, 5, 256, 128], P(None, 'freq', None, 'plane')
- forcing_out: float32 [2, 32, 5, 256, 128], P(None, 'freq', None, 'plane')
All inputs are finite; a program needn't handle non-finite values.
Results may differ from a plain program's by a relative error of at most 0.0003.
Values sent between devices are 32-bit elements; how exact they have to be, the bound alone decides.
A program may use at most 128 MiB of HBM per device.

v0:
```python
import functools
import math

import jax
import jax.numpy as jnp
import numpy as np
from jax import lax
from jax.experimental import pallas as pl
from jax.experimental.pallas import tpu as pltpu
from jax.sharding import PartitionSpec as P

SWEEPS = 4
STEPS = 2


SIDE_WEIGHT = 1.25
MARCH_WEIGHT = 4.0
DIAG_SHIFT = 4.0
ADVECT_SCALE = 0.5
BASE_SCALE = 0.5
HIGHEST_MODE = lax.Precision.HIGHEST


def radial_tables(radius_count):
    indices = np.arange(radius_count)
    angles = math.pi * indices / (radius_count - 1)
    nodes = np.cos(angles)
    weights = np.where((indices == 0) | (indices == radius_count - 1), 2.0, 1.0)
    parity = 1.0 - 2.0 * ((indices[:, None] + indices[None, :]) % 2)
    offdiag = indices[:, None] != indices[None, :]
    spacing = np.where(offdiag, nodes[:, None] - nodes[None, :], 1.0)
    entries = np.where(offdiag, weights[:, None] / weights[None, :] * parity / spacing, 0.0)
    entries = entries - np.diag(entries.sum(axis=1))
    slopes = np.sin(angles)[:, None] * entries / (radius_count - 1)
    system = slopes.T @ slopes + DIAG_SHIFT * np.eye(radius_count)
    return slopes.astype(np.float32), np.linalg.inv(system).astype(np.float32)


def transform_tables(mode_ids, freqs, ntime):
    time_ids = np.arange(ntime)
    angles = 2.0 * math.pi * (mode_ids[:, None] * time_ids[None, :] % ntime) / ntime
    stacked = np.stack([np.cos(angles), -np.sin(angles)])
    return (
        (stacked / math.sqrt(freqs)).astype(np.float32),
        (stacked / math.sqrt(ntime)).astype(np.float32),
    )


def chevron(lobe_count, azimuths, start_az, total_az):
    position = start_az + jnp.arange(azimuths)
    phases = lobe_count[0] * position % total_az
    return 1.0 + 0.5 * jnp.cos(2.0 * math.pi * phases.astype(jnp.float32) / total_az)


def block_of(f, p, nf):
    j = f
    if nf % 4 == 0:
        z, y, x = f // 4, (f // 2) % 2, f % 2
        r = 2 * y + (x + y) % 2
        j = 4 * z + r + (z % 2) * (3 - 2 * r)
    return j + (p % 2) * (nf - 1 - 2 * j)


def freq_of(block, p, nf):
    j = block + (p % 2) * (nf - 1 - 2 * block)
    if nf % 4 == 0:
        z, r = j // 4, j % 4
        r = r + (z % 2) * (3 - 2 * r)
        y = r // 2
        return 4 * z + 2 * y + (r + y) % 2
    return j


def march(
    dims,
    station_ref,
    shape_ref,
    s_state,
    s_base,
    s_forcing,
    omega_ref,
    qt_ref,
    st_ref,
    inv_ref,
    fwd_ref,
    g_state,
    g_forcing,
    r_state,
    r_base,
    r_forcing,
    x_ref,
    b_ref,
    f_ref,
    w_ref,
    o_state,
    o_forcing,
    send_sem,
    recv_sem,
    own_sem,
    halo_send,
    halo_recv,
):
    nf, planes, own_az, variables, per_dev, radii, stored, rows, base_rows = dims
    freqs = nf * per_dev
    ntime = inv_ref.shape[0]
    half = variables * freqs
    me = lax.axis_index("freq")
    plane = lax.axis_index("plane")
    block = block_of(me, plane, nf)
    ring = nf * planes
    here = plane * nf + block
    right, left = (here + 1) % ring, (here + ring - 1) % ring

    def at_ring(g):
        p = g // nf
        return {"freq": freq_of(g % nf, p, nf), "plane": p}

    right_id, left_id = at_ring(right), at_ring(left)

    barrier = pltpu.get_barrier_semaphore()

    @pl.loop(1, nf)
    def _(d):
        pl.semaphore_signal(
            barrier, inc=1, device_id={"freq": (me + d) % nf, "plane": plane}, device_id_type=MESH
        )

    for target in (right_id, left_id):
        pl.semaphore_signal(barrier, inc=1, device_id=target, device_id_type=MESH)
    pl.semaphore_wait(barrier, nf + 1)

    def exchange(k, source, landing, index_to, mine, size, first):
        def copy(d):
            other = (me + d) % nf
            src = source.at[pl.ds(pl.multiple_of(index_to(other) * size, 8), size), :]
            dst = landing.at[pl.ds(pl.multiple_of(mine * size, 8), size), :]
            return pltpu.make_async_remote_copy(
                src_ref=src,
                dst_ref=dst,
                send_sem=send_sem.at[k, d],
                recv_sem=recv_sem.at[k, d],
                device_id={"freq": other, "plane": plane},
                device_id_type=MESH,
            )

        own = pltpu.make_async_copy(
            source.at[pl.ds(pl.multiple_of(index_to(me) * size, 8), size), :],
            landing.at[pl.ds(pl.multiple_of(mine * size, 8), size), :],
            own_sem.at[k],
        )
        if first:

            @pl.loop(1, nf)
            def _(d):
                copy(d).start()

            own.start()
        else:

            @pl.loop(1, nf)
            def _(d):
                copy(d).wait()

            own.wait()

    def to_block(f):
        return block_of(f, plane, nf)

    def to_freq(f):
        return f

    base_args = (1, s_base, r_base, to_block, me, base_rows)
    state_args = (0, s_state, r_state, to_block, me, rows)
    forcing_args = (2, s_forcing, r_forcing, to_block, me, rows)
    out_state_args = (3, o_state, g_state, to_freq, block, rows)
    out_forcing_args = (4, o_forcing, g_forcing, to_freq, block, rows)
    for args in (state_args, base_args, forcing_args):
        exchange(*args, True)

    def halo_copies(e):
        slot = e % 2
        return (
            pltpu.make_async_remote_copy(
                src_ref=x_ref.at[slot, own_az],
                dst_ref=x_ref.at[slot, 0],
                send_sem=halo_send.at[0, e],
                recv_sem=halo_recv.at[0, e],
                device_id=right_id,
                device_id_type=MESH,
            ),
            pltpu.make_async_remote_copy(
                src_ref=x_ref.at[slot, 1],
                dst_ref=x_ref.at[slot, own_az + 1],
                send_sem=halo_send.at[1, e],
                recv_sem=halo_recv.at[1, e],
                device_id=left_id,
                device_id_type=MESH,
            ),
        )

    def place(a, c, v, kk):
        return ((c * variables + v) * per_dev + kk) * nf

    def packed_row(a, c, v, kk):
        return ((c * per_dev + kk) * variables + v) * own_az + a

    def each_run(visit):
        @pl.loop(0, own_az)
        def _(a):
            for c in range(2):
                for v in range(variables):
                    for kk in range(per_dev):
                        visit(a, place(a, c, v, kk), packed_row(a, c, v, kk))

    exchange(*state_args, False)

    def unpack_state(a, start, row):
        x_ref[0, a + 1, pl.ds(start, nf), :] = r_state[pl.ds(row, nf, stride=rows), :]

    each_run(unpack_state)
    for copy in halo_copies(0):
        copy.start()
    exchange(*base_args, False)
    exchange(*forcing_args, False)

    def unpack_forcing(a, start, row):
        b_ref[a, pl.ds(start, nf), :] = (
            MARCH_WEIGHT * x_ref[0, a + 1, pl.ds(start, nf), :]
            + r_forcing[pl.ds(row, nf, stride=rows), :]
        )

    each_run(unpack_forcing)
    omega = omega_ref[...][None]
    flat = (2 * half, radii)
    cube = (variables, freqs, radii)

    def sweep_slab(src, dst, a):
        x = x_ref[src, a + 1]
        beside = SIDE_WEIGHT * (x_ref[src, a] + x_ref[src, a + 2]) + b_ref[a]
        real, imag = x[:half].reshape(cube), x[half:].reshape(cube)
        w = w_ref[a][:variables][:, None, :]
        mixing = jnp.concatenate([w * real - omega * imag, w * imag + omega * real], axis=0)
        summed = beside - mixing.reshape(flat)
        x_ref[dst, a + 1] = jnp.dot(
            summed, qt_ref[...], precision=HIGHEST_MODE, preferred_element_type=jnp.float32
        )

    def advect_slab(slot, a, final):
        x = x_ref[slot, a + 1]
        beside = 0.5 * (x_ref[slot, a + 2] - x_ref[slot, a])

        def lanes(y):
            return [
                jnp.concatenate(
                    [
                        y[v * freqs : (v + 1) * freqs],
                        y[half + v * freqs : half + (v + 1) * freqs],
                    ],
                    axis=0,
                )
                for v in range(variables)
            ]

        both = jnp.concatenate(lanes(x) + lanes(beside), axis=1)
        in_time = jnp.dot(
            inv_ref[...], both, precision=HIGHEST_MODE, preferred_element_type=jnp.float32
        )
        u = [in_time[:, v * radii : (v + 1) * radii] for v in range(variables)]
        ua = [
            in_time[:, (variables + v) * radii : (variables + v + 1) * radii]
            for v in range(variables)
        ]
        radial = jnp.dot(
            jnp.concatenate(u, axis=0),
            st_ref[...],
            precision=HIGHEST_MODE,
            preferred_element_type=jnp.float32,
        )
        ur = [radial[v * ntime : (v + 1) * ntime] for v in range(variables)]
        n = [u[1] * ur[v] + u[2] * ua[v] for v in range(variables)]
        n[0] = n[0] + u[0] * (ur[1] + ua[2])
        source = -ADVECT_SCALE * jnp.concatenate(n, axis=1)
        spectral = jnp.dot(
            fwd_ref[...], source, precision=HIGHEST_MODE, preferred_element_type=jnp.float32
        )
        forcing = jnp.concatenate(
            [
                spectral[c * freqs : (c + 1) * freqs, v * radii : (v + 1) * radii]
                for c in range(2)
                for v in range(variables)
            ],
            axis=0,
        )
        if final:
            f_ref[a] = forcing
        else:
            b_ref[a] = MARCH_WEIGHT * x + forcing

    for station in range(STEPS):
        wanted = station_ref[station]

        @pl.loop(0, own_az)
        def _(a):
            for v in range(variables):
                w_ref[a, pl.ds(v, 1), :] = (BASE_SCALE * shape_ref[a]) * r_base[
                    pl.ds(
                        (wanted // stored) * base_rows
                        + ((wanted % stored) * variables + v) * own_az
                        + a,
                        1,
                    ),
                    :,
                ]

        @pl.loop(0, SWEEPS)
        def _(sweep):
            e = station * SWEEPS + sweep
            src, dst = e % 2, (e + 1) % 2

            @pl.when((sweep > 0) | (station == 0))
            def _():
                for copy in halo_copies(e):
                    copy.wait()

            sweep_slab(src, dst, 0)
            if own_az > 1:
                sweep_slab(src, dst, own_az - 1)
            for copy in halo_copies(e + 1):
                copy.start()

            @pl.loop(1, own_az - 1)
            def _(a):
                sweep_slab(src, dst, a)

        last = (station + 1) * SWEEPS
        slot = last % 2
        final = station == STEPS - 1
        if final:

            def pack_state(a, start, row):
                o_state[pl.ds(row, nf, stride=rows), :] = x_ref[slot, a + 1, pl.ds(start, nf), :]

            each_run(pack_state)
            exchange(*out_state_args, True)

        @pl.loop(1, own_az - 1)
        def _(a):
            advect_slab(slot, a, final)

        for copy in halo_copies(last):
            copy.wait()
        advect_slab(slot, 0, final)
        if own_az > 1:
            advect_slab(slot, own_az - 1, final)

    def pack_forcing(a, start, row):
        o_forcing[pl.ds(row, nf, stride=rows), :] = f_ref[a, pl.ds(start, nf), :]

    each_run(pack_forcing)
    exchange(*out_forcing_args, True)
    exchange(*out_state_args, False)
    exchange(*out_forcing_args, False)


def per_device(state_in, forcing_in, base_flow, station_index, lobe_count):
    _, per_dev, variables, span_az, radii = state_in.shape
    nf = lax.axis_size("freq")
    planes = lax.axis_size("plane")
    freqs = per_dev * nf
    ntime = 3 * freqs // 2
    own_az = span_az // nf
    stored = base_flow.shape[0]
    slopes, inverse_p = radial_tables(radii)
    mode_ids = (np.arange(nf)[None, :] * per_dev + np.arange(per_dev)[:, None]).reshape(-1)
    inverse, forward = transform_tables(mode_ids, freqs, ntime)
    omegas = np.broadcast_to((0.5 * mode_ids / freqs).astype(np.float32)[:, None], (freqs, radii))
    plane = lax.axis_index("plane")
    block = block_of(lax.axis_index("freq"), plane, nf)
    shape_az = chevron(lobe_count, own_az, plane * span_az + block * own_az, span_az * planes)

    def padded_rows(count):
        return -(-count // 8) * 8

    def chunks(x, size):
        x = x.reshape(-1, nf, own_az, radii).transpose(1, 0, 2, 3).reshape(nf, -1, radii)
        x = jnp.pad(x, ((0, 0), (0, size - x.shape[1]), (0, 0)))
        return x.reshape(nf * size, radii)

    count = 2 * per_dev * variables * own_az
    rows = padded_rows(count)
    base_rows = padded_rows(stored * variables * own_az)
    dims = (nf, planes, own_az, variables, per_dev, radii, stored, rows, base_rows)
    half = variables * freqs
    exchanges = STEPS * SWEEPS + 1
    vmem = pl.BlockSpec(memory_space=pltpu.VMEM)
    smem = pl.BlockSpec(memory_space=pltpu.SMEM)
    anywhere = pl.BlockSpec(memory_space=pl.ANY)
    packed = (nf * rows, radii)
    f32 = jnp.float32
    outs = pl.pallas_call(
        functools.partial(march, dims),
        out_shape=[jax.ShapeDtypeStruct(packed, f32)] * 2,
        in_specs=[smem, smem, anywhere, anywhere, anywhere] + [vmem] * 5,
        out_specs=[anywhere, anywhere],
        scratch_shapes=[
            pltpu.VMEM(packed, f32),
            pltpu.VMEM((nf * base_rows, radii), f32),
            pltpu.VMEM(packed, f32),
            pltpu.VMEM((2, own_az + 2, 2 * half, radii), f32),
            pltpu.VMEM((own_az, 2 * half, radii), f32),
            pltpu.VMEM((own_az, 2 * half, radii), f32),
            pltpu.VMEM((own_az, padded_rows(variables), radii), f32),
            pltpu.VMEM(packed, f32),
            pltpu.VMEM(packed, f32),
            pltpu.SemaphoreType.DMA((5, nf)),
            pltpu.SemaphoreType.DMA((5, nf)),
            pltpu.SemaphoreType.DMA((5,)),
            pltpu.SemaphoreType.DMA((2, exchanges)),
            pltpu.SemaphoreType.DMA((2, exchanges)),
        ],
        compiler_params=pltpu.CompilerParams(
            collective_id=0, has_side_effects=True, vmem_limit_bytes=48 * 1024 * 1024
        ),
    )(
        station_index,
        shape_az,
        chunks(state_in, rows),
        chunks(base_flow, base_rows),
        chunks(forcing_in, rows),
        jnp.asarray(omegas),
        jnp.asarray(inverse_p.T),
        jnp.asarray(slopes.T),
        jnp.asarray(inverse.transpose(2, 0, 1).reshape(ntime, 2 * freqs)),
        jnp.asarray(forward.reshape(2 * freqs, ntime)),
    )

    return tuple(finish(y, nf, per_dev, variables, own_az, radii, rows, count) for y in outs)


def finish(y, nf, per_dev, variables, own_az, radii, rows, count):
    y = y.reshape(nf, rows, radii)[:, :count].reshape(nf, -1, own_az, radii)
    return y.transpose(1, 0, 2, 3).reshape(2, per_dev, variables, nf * own_az, radii)


MESH = pl.DeviceIdType.MESH


def solution(mesh):
    return jax.shard_map(
        per_device,
        mesh=mesh,
        in_specs=(
            P(None, "freq", None, "plane", None),
            P(None, "freq", None, "plane", None),
            P("freq", None, "plane", None),
            P(),
            P(),
        ),
        out_specs=(P(None, "freq", None, "plane", None), P(None, "freq", None, "plane", None)),
        check_vma=False,
    )
```

profile of v0, /device:TPU:14, one launch (start us, length us, event | category | flops | bytes accessed | tf_op | source)
XLA Modules:
  0.0 184.0 jit_solution(16939033067202710494)
XLA Ops:
  1.4 0.1 fusion.4.shape_ref
  1.4 1.0 copy.13
  2.4 0.0 copy-start.5
  2.4 1.5 copy.12
  4.0 0.1 copy-done.5
  4.1 0.0 copy-start.6
  4.1 0.0 copy-start
  4.1 0.0 copy-start.1
  4.1 0.0 copy-start.2
  4.1 0.0 copy-start.3
  4.2 0.0 copy-start.4
  4.2 0.1 copy.14
  4.3 0.5 copy-done.6
  4.8 0.1 jit_solution_.3.omega_ref
  4.9 0.1 copy-done
  5.0 0.0 copy-done.1
  5.0 0.0 copy-done.2
  5.0 0.0 copy-done.3
  5.0 0.0 copy-done.4
  5.0 176.6 %shard_map.113 = (f32[2560,128]{1,0:T(8,128)S(1)}, f32[2560,128]{1,0:T(8,128)S(1)}) custom-call(s32[2]{0:T(128)S(1)} %copy-done.4, f32[8]{0:T(128)S(1)} %fusion.4.shape_ref, f32[2560,128]{1,0:T(8,128)S(1)} %bitcast.22, f32[640,128]{1,0:T(8,128)S(1)} %bitcast.26, f32[2560,128]{1,0:T(8,128)S(1)} %bitcast.23, f32[32,128]{1,0:T(8,128)S(1)} %jit_solution_.3.omega_ref, ...), custom_call_target="tpu_custom_call" | custom-call | tf_op jit(solution)/shard_map/pallas_call | solution.py:400
  181.6 1.2 copy.15
  182.8 1.2 copy.16
Async XLA Ops:
  2.4 1.7 copy-start.5
  4.1 0.7 copy-start.6
  4.1 0.9 copy-start
  4.1 0.9 copy-start.1
  4.1 0.9 copy-start.2
  4.1 0.9 copy-start.3
  4.2 0.9 copy-start.4
where the time goes:
time: 184 us
  Pallas kernels  177 us (96%)
  local copies, waits for them, and re-layouts  5.96 us (3%)
    pallas_call x1, Pallas kernels, per_device(): pl.pallas_call(functools.partial(march, dims), out_shape=[jax.ShapeDtypeS...  177 us

commit v1 on v0

--- a/solution.py
+++ b/solution.py
@@ -18,7 +18,6 @@
 DIAG_SHIFT = 4.0
 ADVECT_SCALE = 0.5
 BASE_SCALE = 0.5
-HIGHEST_MODE = lax.Precision.HIGHEST
 
 
 def radial_tables(radius_count):
@@ -52,6 +51,41 @@
     return 1.0 + 0.5 * jnp.cos(2.0 * math.pi * phases.astype(jnp.float32) / total_az)
 
 
+def halves(x):
+    high = x.astype(jnp.bfloat16)
+    return high, (x - high.astype(jnp.float32)).astype(jnp.bfloat16)
+
+
+def right_table(table):
+    high, low = np_halves(table)
+    return jnp.asarray(np.tile(np.concatenate([high, low], axis=1), (2, 1)))
+
+
+def left_table(table):
+    high, low = np_halves(table)
+    return jnp.asarray(np.concatenate([high, high, low, low], axis=1))
+
+
+def np_halves(table):
+    high = table.astype(jnp.bfloat16)
+    return high, (table - high.astype(np.float32)).astype(jnp.bfloat16)
+
+
+def times_right(x, table):
+    width = table.shape[1] // 2
+    y = jnp.dot(jnp.concatenate(halves(x), axis=1), table, preferred_element_type=jnp.float32)
+    return y[:, :width] + y[:, width:]
+
+
+def times_left(table, x):
+    high, low = halves(x)
+    return jnp.dot(
+        table,
+        jnp.concatenate([high, low, high, low], axis=0),
+        preferred_element_type=jnp.float32,
+    )
+
+
 def block_of(f, p, nf):
     j = f
     if nf % 4 == 0:
@@ -75,9 +109,10 @@
     dims,
     station_ref,
     shape_ref,
-    s_state,
+    rate_ref,
+    state_ref,
     s_base,
-    s_forcing,
+    forcing_ref,
     omega_ref,
     qt_ref,
     st_ref,
@@ -87,7 +122,14 @@
     g_forcing,
     r_state,
     r_base,
-    r_forcing,
+    s_state,
+    s_w,
+    r_w,
+    plane_w,
+    x_one,
+    b_one,
+    edge_out,
+    edge_in,
     x_ref,
     b_ref,
     f_ref,
@@ -99,9 +141,14 @@
     own_sem,
     halo_send,
     halo_recv,
+    edge_send,
+    edge_recv,
+    load_sem,
 ):
-    nf, planes, own_az, variables, per_dev, radii, stored, rows, base_rows = dims
+    nf, planes, own_az, variables, per_dev, radii, stored, rows, base_rows, w_rows = dims
     freqs = nf * per_dev
+    span = nf * own_az
+    runs = 2 * per_dev * variables
     ntime = inv_ref.shape[0]
     half = variables * freqs
     me = lax.axis_index("freq")
@@ -125,9 +172,15 @@
             barrier, inc=1, device_id={"freq": (me + d) % nf, "plane": plane}, device_id_type=MESH
         )
 
-    for target in (right_id, left_id):
+    beyond = {"freq": me, "plane": (plane + 1) % planes}
+    behind = {"freq": me, "plane": (plane + planes - 1) % planes}
+    for target in (right_id, left_id, beyond, behind):
         pl.semaphore_signal(barrier, inc=1, device_id=target, device_id_type=MESH)
-    pl.semaphore_wait(barrier, nf + 1)
+    load_state = pltpu.make_async_copy(state_ref, x_one.at[0, :, pl.ds(8, span), :], load_sem.at[0])
+    load_forcing = pltpu.make_async_copy(forcing_ref, b_one, load_sem.at[1])
+    load_state.start()
+    load_forcing.start()
+    pl.semaphore_wait(barrier, nf + 3)
 
     def exchange(k, source, landing, index_to, mine, size, first):
         def copy(d):
@@ -171,11 +224,10 @@
 
     base_args = (1, s_base, r_base, to_block, me, base_rows)
     state_args = (0, s_state, r_state, to_block, me, rows)
-    forcing_args = (2, s_forcing, r_forcing, to_block, me, rows)
+    w_args = (2, s_w, r_w, lambda f: 0, block, w_rows)
     out_state_args = (3, o_state, g_state, to_freq, block, rows)
     out_forcing_args = (4, o_forcing, g_forcing, to_freq, block, rows)
-    for args in (state_args, base_args, forcing_args):
-        exchange(*args, True)
+    exchange(*base_args, True)
 
     def halo_copies(e):
         slot = e % 2
@@ -212,6 +264,109 @@
                     for kk in range(per_dev):
                         visit(a, place(a, c, v, kk), packed_row(a, c, v, kk))
 
+    def in_row(a, c, v, kk):
+        return ((c * per_dev + kk) * variables + v) * own_az + a
+
+    def edge_copies(e):
+        return [
+            pltpu.make_async_remote_copy(
+                src_ref=edge_out.at[e, side],
+                dst_ref=edge_in.at[e, side],
+                send_sem=edge_send.at[side, e],
+                recv_sem=edge_recv.at[side, e],
+                device_id=target,
+                device_id_type=MESH,
+            )
+            for side, target in ((0, beyond), (1, behind))
+        ]
+
+    def send_edges(slot, e):
+        for m in range(runs):
+            edge_out[e, 0, pl.ds(m, 1), :] = x_one[slot, m, pl.ds(7 + span, 1), :]
+            edge_out[e, 1, pl.ds(m, 1), :] = x_one[slot, m, pl.ds(8, 1), :]
+        for copy in edge_copies(e):
+            copy.start()
+
+    load_state.wait()
+    send_edges(0, 0)
+    load_forcing.wait()
+
+    @pl.loop(0, runs)
+    def _(m):
+        b_one[m] = MARCH_WEIGHT * x_one[0, m, pl.ds(8, span), :] + b_one[m]
+
+    exchange(*base_args, False)
+    for station in range(STEPS):
+        wanted = station_ref[station]
+
+        @pl.loop(0, own_az)
+        def _(a):
+            for v in range(variables):
+                scaled = (BASE_SCALE * shape_ref[a]) * r_base[
+                    pl.ds(
+                        (wanted // stored) * base_rows
+                        + ((wanted % stored) * variables + v) * own_az
+                        + a,
+                        1,
+                    ),
+                    :,
+                ]
+                if station == 0:
+                    s_w[pl.ds(v * own_az + a, 1), :] = scaled
+                else:
+                    w_ref[(station - 1) * own_az + a, pl.ds(v, 1), :] = scaled
+
+        if station == 0:
+            exchange(*w_args, True)
+    exchange(*w_args, False)
+
+    @pl.loop(0, nf)
+    def _(j):
+        for v in range(variables):
+            plane_w[v, pl.ds(j * own_az, own_az), :] = r_w[pl.ds(j * w_rows + v * own_az, own_az), :]
+
+    @pl.loop(0, SWEEPS)
+    def _(e):
+        src, dst = e % 2, (e + 1) % 2
+        for copy in edge_copies(e):
+            copy.wait()
+        for m in range(runs):
+            x_one[src, m, pl.ds(7, 1), :] = edge_in[e, 0, pl.ds(m, 1), :]
+            x_one[src, m, pl.ds(8 + span, 1), :] = edge_in[e, 1, pl.ds(m, 1), :]
+        for kk in range(per_dev):
+            rate = rate_ref[kk]
+
+            @pl.loop(0, variables)
+            def _(v):
+                w = plane_w[v]
+                at = [(c * per_dev + kk) * variables + v for c in range(2)]
+                real, imag = [x_one[src, m, pl.ds(8, span), :] for m in at]
+                mixing = (w * real - rate * imag, w * imag + rate * real)
+                summed = [
+                    SIDE_WEIGHT
+                    * (x_one[src, m, pl.ds(7, span), :] + x_one[src, m, pl.ds(9, span), :])
+                    + b_one[m]
+                    - mixed
+                    for m, mixed in zip(at, mixing)
+                ]
+                q = times_right(jnp.concatenate(summed, axis=0), qt_ref[...])
+                x_one[dst, at[0], pl.ds(8, span), :] = q[:span]
+                x_one[dst, at[1], pl.ds(8, span), :] = q[span:]
+
+        @pl.when(e < SWEEPS - 1)
+        def _():
+            send_edges(dst, e + 1)
+
+    settled = SWEEPS % 2
+
+    @pl.loop(0, nf)
+    def _(j):
+        for m in range(runs):
+            s_state[pl.ds(j * rows + m * own_az, own_az), :] = x_one[
+                settled, m, pl.ds(8 + j * own_az, own_az), :
+            ]
+
+    exchange(*state_args, True)
     exchange(*state_args, False)
 
     def unpack_state(a, start, row):
@@ -220,30 +375,18 @@
     each_run(unpack_state)
     for copy in halo_copies(0):
         copy.start()
-    exchange(*base_args, False)
-    exchange(*forcing_args, False)
-
-    def unpack_forcing(a, start, row):
-        b_ref[a, pl.ds(start, nf), :] = (
-            MARCH_WEIGHT * x_ref[0, a + 1, pl.ds(start, nf), :]
-            + r_forcing[pl.ds(row, nf, stride=rows), :]
-        )
-
-    each_run(unpack_forcing)
     omega = omega_ref[...][None]
     flat = (2 * half, radii)
     cube = (variables, freqs, radii)
 
-    def sweep_slab(src, dst, a):
+    def sweep_slab(src, dst, a, station):
         x = x_ref[src, a + 1]
         beside = SIDE_WEIGHT * (x_ref[src, a] + x_ref[src, a + 2]) + b_ref[a]
         real, imag = x[:half].reshape(cube), x[half:].reshape(cube)
-        w = w_ref[a][:variables][:, None, :]
+        w = w_ref[(station - 1) * own_az + a][:variables][:, None, :]
         mixing = jnp.concatenate([w * real - omega * imag, w * imag + omega * real], axis=0)
         summed = beside - mixing.reshape(flat)
-        x_ref[dst, a + 1] = jnp.dot(
-            summed, qt_ref[...], precision=HIGHEST_MODE, preferred_element_type=jnp.float32
-        )
+        x_ref[dst, a + 1] = times_right(summed, qt_ref[...])
 
     def advect_slab(slot, a, final):
         x = x_ref[slot, a + 1]
@@ -262,27 +405,18 @@
             ]
 
         both = jnp.concatenate(lanes(x) + lanes(beside), axis=1)
-        in_time = jnp.dot(
-            inv_ref[...], both, precision=HIGHEST_MODE, preferred_element_type=jnp.float32
-        )
+        in_time = times_left(inv_ref[...], both)
         u = [in_time[:, v * radii : (v + 1) * radii] for v in range(variables)]
         ua = [
             in_time[:, (variables + v) * radii : (variables + v + 1) * radii]
             for v in range(variables)
         ]
-        radial = jnp.dot(
-            jnp.concatenate(u, axis=0),
-            st_ref[...],
-            precision=HIGHEST_MODE,
-            preferred_element_type=jnp.float32,
-        )
+        radial = times_right(jnp.concatenate(u, axis=0), st_ref[...])
         ur = [radial[v * ntime : (v + 1) * ntime] for v in range(variables)]
         n = [u[1] * ur[v] + u[2] * ua[v] for v in range(variables)]
         n[0] = n[0] + u[0] * (ur[1] + ua[2])
         source = -ADVECT_SCALE * jnp.concatenate(n, axis=1)
-        spectral = jnp.dot(
-            fwd_ref[...], source, precision=HIGHEST_MODE, preferred_element_type=jnp.float32
-        )
+        spectral = times_left(fwd_ref[...], source)
         forcing = jnp.concatenate(
             [
                 spectral[c * freqs : (c + 1) * freqs, v * radii : (v + 1) * radii]
@@ -296,62 +430,52 @@
         else:
             b_ref[a] = MARCH_WEIGHT * x + forcing
 
-    for station in range(STEPS):
-        wanted = station_ref[station]
-
-        @pl.loop(0, own_az)
-        def _(a):
-            for v in range(variables):
-                w_ref[a, pl.ds(v, 1), :] = (BASE_SCALE * shape_ref[a]) * r_base[
-                    pl.ds(
-                        (wanted // stored) * base_rows
-                        + ((wanted % stored) * variables + v) * own_az
-                        + a,
-                        1,
-                    ),
-                    :,
-                ]
-
-        @pl.loop(0, SWEEPS)
-        def _(sweep):
-            e = station * SWEEPS + sweep
-            src, dst = e % 2, (e + 1) % 2
-
-            @pl.when((sweep > 0) | (station == 0))
-            def _():
-                for copy in halo_copies(e):
-                    copy.wait()
-
-            sweep_slab(src, dst, 0)
-            if own_az > 1:
-                sweep_slab(src, dst, own_az - 1)
-            for copy in halo_copies(e + 1):
-                copy.start()
-
-            @pl.loop(1, own_az - 1)
-            def _(a):
-                sweep_slab(src, dst, a)
-
-        last = (station + 1) * SWEEPS
-        slot = last % 2
-        final = station == STEPS - 1
-        if final:
-
-            def pack_state(a, start, row):
-                o_state[pl.ds(row, nf, stride=rows), :] = x_ref[slot, a + 1, pl.ds(start, nf), :]
-
-            each_run(pack_state)
-            exchange(*out_state_args, True)
-
+    def advect_all(slot, e, final):
         @pl.loop(1, own_az - 1)
         def _(a):
             advect_slab(slot, a, final)
 
-        for copy in halo_copies(last):
+        for copy in halo_copies(e):
             copy.wait()
         advect_slab(slot, 0, final)
         if own_az > 1:
             advect_slab(slot, own_az - 1, final)
+
+    advect_all(0, 0, False)
+    for station in range(1, STEPS):
+
+        @pl.loop(0, SWEEPS)
+        def _(sweep):
+            e = (station - 1) * SWEEPS + sweep
+            src, dst = e % 2, (e + 1) % 2
+
+            @pl.when(sweep > 0)
+            def _():
+                for copy in halo_copies(e):
+                    copy.wait()
+
+            sweep_slab(src, dst, 0, station)
+            if own_az > 1:
+                sweep_slab(src, dst, own_az - 1, station)
+            for copy in halo_copies(e + 1):
+                copy.start()
+
+            @pl.loop(1, own_az - 1)
+            def _(a):
+                sweep_slab(src, dst, a, station)
+
+        last = station * SWEEPS
+        slot = last % 2
+        final = station == STEPS - 1
+        if final:
+
+            def pack_state(a, start, row):
+                o_state[pl.ds(row, nf, stride=rows), :] = x_ref[slot, a + 1, pl.ds(start, nf), :]
+
+            each_run(pack_state)
+            exchange(*out_state_args, True)
+
+        advect_all(slot, last, final)
 
     def pack_forcing(a, start, row):
         o_forcing[pl.ds(row, nf, stride=rows), :] = f_ref[a, pl.ds(start, nf), :]
@@ -389,9 +513,14 @@
     count = 2 * per_dev * variables * own_az
     rows = padded_rows(count)
     base_rows = padded_rows(stored * variables * own_az)
-    dims = (nf, planes, own_az, variables, per_dev, radii, stored, rows, base_rows)
+    w_rows = padded_rows(variables * own_az)
+    dims = (nf, planes, own_az, variables, per_dev, radii, stored, rows, base_rows, w_rows)
     half = variables * freqs
-    exchanges = STEPS * SWEEPS + 1
+    exchanges = (STEPS - 1) * SWEEPS + 1
+    runs = 2 * per_dev * variables
+    edge_rows = padded_rows(runs)
+    first_mode = lax.axis_index("freq") * per_dev
+    rates = 0.5 * (first_mode + jnp.arange(per_dev)).astype(jnp.float32) / freqs
     vmem = pl.BlockSpec(memory_space=pltpu.VMEM)
     smem = pl.BlockSpec(memory_space=pltpu.SMEM)
     anywhere = pl.BlockSpec(memory_space=pl.ANY)
@@ -400,16 +529,23 @@
     outs = pl.pallas_call(
         functools.partial(march, dims),
         out_shape=[jax.ShapeDtypeStruct(packed, f32)] * 2,
-        in_specs=[smem, smem, anywhere, anywhere, anywhere] + [vmem] * 5,
+        in_specs=[smem, smem, smem, anywhere, anywhere, anywhere] + [vmem] * 5,
         out_specs=[anywhere, anywhere],
         scratch_shapes=[
             pltpu.VMEM(packed, f32),
             pltpu.VMEM((nf * base_rows, radii), f32),
             pltpu.VMEM(packed, f32),
+            pltpu.VMEM((w_rows, radii), f32),
+            pltpu.VMEM((nf * w_rows, radii), f32),
+            pltpu.VMEM((variables, span_az, radii), f32),
+            pltpu.VMEM((2, runs, span_az + 16, radii), f32),
+            pltpu.VMEM((runs, span_az, radii), f32),
+            pltpu.VMEM((SWEEPS, 2, edge_rows, radii), f32),
+            pltpu.VMEM((SWEEPS, 2, edge_rows, radii), f32),
             pltpu.VMEM((2, own_az + 2, 2 * half, radii), f32),
             pltpu.VMEM((own_az, 2 * half, radii), f32),
             pltpu.VMEM((own_az, 2 * half, radii), f32),
-            pltpu.VMEM((own_az, padded_rows(variables), radii), f32),
+            pltpu.VMEM(((STEPS - 1) * own_az, padded_rows(variables), radii), f32),
             pltpu.VMEM(packed, f32),
             pltpu.VMEM(packed, f32),
             pltpu.SemaphoreType.DMA((5, nf)),
@@ -417,6 +553,9 @@
             pltpu.SemaphoreType.DMA((5,)),
             pltpu.SemaphoreType.DMA((2, exchanges)),
             pltpu.SemaphoreType.DMA((2, exchanges)),
+            pltpu.SemaphoreType.DMA((2, SWEEPS)),
+            pltpu.SemaphoreType.DMA((2, SWEEPS)),
+            pltpu.SemaphoreType.DMA((2,)),
         ],
         compiler_params=pltpu.CompilerParams(
             collective_id=0, has_side_effects=True, vmem_limit_bytes=48 * 1024 * 1024
@@ -424,14 +563,15 @@
     )(
         station_index,
         shape_az,
-        chunks(state_in, rows),
+        rates,
+        state_in.reshape(runs, span_az, radii),
         chunks(base_flow, base_rows),
-        chunks(forcing_in, rows),
+        forcing_in.reshape(runs, span_az, radii),
         jnp.asarray(omegas),
-        jnp.asarray(inverse_p.T),
-        jnp.asarray(slopes.T),
-        jnp.asarray(inverse.transpose(2, 0, 1).reshape(ntime, 2 * freqs)),
-        jnp.asarray(forward.reshape(2 * freqs, ntime)),
+        right_table(inverse_p.T),
+        right_table(slopes.T),
+        left_table(inverse.transpose(2, 0, 1).reshape(ntime, 2 * freqs)),
+        left_table(forward.reshape(2 * freqs, ntime)),
     )
 
     return tuple(finish(y, nf, per_dev, variables, own_az, radii, rows, count) for y in outs)

time: 184 us -> 164 us (0.89)
  Pallas kernels: 177 us -> 152 us
  local copies, waits for them, and re-layouts: 5.96 us -> 10.7 us
    pallas_call x1, Pallas kernels: 177 us -> 152 us  [per_device(): pl.pallas_call(functools.partial(march, dims), out_shape=[jax.ShapeDtypeS...]
    unnamed x14, local copies, waits for them, and re-layouts: 0.82 us -> 6.59 us
where the time goes in v1:
time: 164 us
  Pallas kernels  152 us (93%)
  local copies, waits for them, and re-layouts  10.7 us (7%)
    pallas_call x1, Pallas kernels, per_device(): pl.pallas_call(functools.partial(march, dims), out_shape=[jax.ShapeDtypeS...  152 us
    unnamed x14, local copies, waits for them, and re-layouts  6.59 us

profile of v1, /device:TPU:14, one launch (start us, length us, event | category | flops | bytes accessed | tf_op | source)
XLA Modules:
  0.0 163.9 jit_solution(1490290363252838406)
XLA Ops:
  1.4 0.1 fusion.4.shape_ref
  1.4 1.0 copy.12
  2.4 0.7 jit_solution_.3.omega_ref
  3.2 0.0 copy-start
  3.2 1.3 copy-done
  4.5 0.0 copy-start.1
  4.5 1.3 copy-done.1
  5.8 0.0 copy-start.2
  5.8 0.9 copy-done.2
  6.7 0.0 copy-start.3
  6.7 0.9 copy-done.3
  7.6 0.0 copy-start.4
  7.6 0.8 copy-done.4
  8.4 0.0 copy-start.5
  8.4 0.7 copy-done.5
  9.1 0.0 copy-start.6
  9.1 0.7 copy-done.6
  9.8 151.7 %shard_map.113 = (f32[2560,128]{1,0:T(8,128)S(1)}, f32[2560,128]{1,0:T(8,128)S(1)}) custom-call(s32[2]{0:T(128)S(1)} %copy-done.6, f32[8]{0:T(128)S(1)} %fusion.4.shape_ref, f32[2]{0:T(128)S(1)} %convert_multiply_fusion.rate_ref, f32[20,128,128]{2,1,0:T(8,128)S(1)} %bitcast.16, f32[640,128]{1,0:T(8,128)S(1)} %bitcast.18, f32[20,128,128]{2,1,0:T(8,128)S(1)} %bitcast.17, ...), custom_call_target="tpu_custom_call" | custom-call | tf_op jit(solution)/shard_map/pallas_call | solution.py:529
  161.5 1.2 copy.13
  162.7 1.2 copy.14
  (1 shorter events, 0.0 us)
Async XLA Ops:
  3.2 1.3 copy-start
  4.5 1.3 copy-start.1
  5.8 0.9 copy-start.2
  6.7 0.9 copy-start.3
  7.6 0.8 copy-start.4
  8.4 0.7 copy-start.5
  9.1 0.7 copy-start.6

commit v2 on v1

--- a/solution.py
+++ b/solution.py
@@ -86,23 +86,26 @@
     )
 
 
-def block_of(f, p, nf):
-    j = f
+def ring_of(f, p, nf, planes):
+    at = f
     if nf % 4 == 0:
+        high = nf // 4
         z, y, x = f // 4, (f // 2) % 2, f % 2
-        r = 2 * y + (x + y) % 2
-        j = 4 * z + r + (z % 2) * (3 - 2 * r)
-    return j + (p % 2) * (nf - 1 - 2 * j)
-
-
-def freq_of(block, p, nf):
-    j = block + (p % 2) * (nf - 1 - 2 * block)
+        column = 2 * y + (x + y) % 2
+        at = column * high + z + (column % 2) * (high - 1 - 2 * z)
+    return at * planes + p
+
+
+def device_of(g, nf, planes):
+    at = g // planes
+    f = at
     if nf % 4 == 0:
-        z, r = j // 4, j % 4
-        r = r + (z % 2) * (3 - 2 * r)
-        y = r // 2
-        return 4 * z + 2 * y + (r + y) % 2
-    return j
+        high = nf // 4
+        column, z = at // high, at % high
+        z = z + (column % 2) * (high - 1 - 2 * z)
+        y = column // 2
+        f = 4 * z + 2 * y + (column + y) % 2
+    return f, g % planes
 
 
 def march(
@@ -113,11 +116,11 @@
     state_ref,
     s_base,
     forcing_ref,
-    omega_ref,
-    qt_ref,
-    st_ref,
-    inv_ref,
-    fwd_ref,
+    far_omega,
+    far_qt,
+    far_st,
+    far_inv,
+    far_fwd,
     g_state,
     g_forcing,
     r_state,
@@ -144,6 +147,12 @@
     edge_send,
     edge_recv,
     load_sem,
+    omega_ref,
+    qt_ref,
+    st_ref,
+    inv_ref,
+    fwd_ref,
+    table_sem,
 ):
     nf, planes, own_az, variables, per_dev, radii, stored, rows, base_rows, w_rows = dims
     freqs = nf * per_dev
@@ -153,80 +162,120 @@
     half = variables * freqs
     me = lax.axis_index("freq")
     plane = lax.axis_index("plane")
-    block = block_of(me, plane, nf)
     ring = nf * planes
-    here = plane * nf + block
-    right, left = (here + 1) % ring, (here + ring - 1) % ring
-
-    def at_ring(g):
-        p = g // nf
-        return {"freq": freq_of(g % nf, p, nf), "plane": p}
-
-    right_id, left_id = at_ring(right), at_ring(left)
-
+    here = ring_of(me, plane, nf, planes)
+    part, block = here // nf, here % nf
+
+    def named(device):
+        return {"freq": device[0], "plane": device[1]}
+
+    right_id = named(device_of((here + 1) % ring, nf, planes))
+    left_id = named(device_of((here + ring - 1) % ring, nf, planes))
     barrier = pltpu.get_barrier_semaphore()
 
-    @pl.loop(1, nf)
+    @pl.loop(1, ring)
     def _(d):
+        other = (me * planes + plane + d) % ring
         pl.semaphore_signal(
-            barrier, inc=1, device_id={"freq": (me + d) % nf, "plane": plane}, device_id_type=MESH
+            barrier,
+            inc=1,
+            device_id={"freq": other // planes, "plane": other % planes},
+            device_id_type=MESH,
         )
 
     beyond = {"freq": me, "plane": (plane + 1) % planes}
     behind = {"freq": me, "plane": (plane + planes - 1) % planes}
-    for target in (right_id, left_id, beyond, behind):
-        pl.semaphore_signal(barrier, inc=1, device_id=target, device_id_type=MESH)
     load_state = pltpu.make_async_copy(state_ref, x_one.at[0, :, pl.ds(8, span), :], load_sem.at[0])
     load_forcing = pltpu.make_async_copy(forcing_ref, b_one, load_sem.at[1])
     load_state.start()
     load_forcing.start()
-    pl.semaphore_wait(barrier, nf + 3)
-
-    def exchange(k, source, landing, index_to, mine, size, first):
-        def copy(d):
-            other = (me + d) % nf
-            src = source.at[pl.ds(pl.multiple_of(index_to(other) * size, 8), size), :]
-            dst = landing.at[pl.ds(pl.multiple_of(mine * size, 8), size), :]
+    tables = [
+        pltpu.make_async_copy(far, near, table_sem.at[i])
+        for i, (far, near) in enumerate(
+            (
+                (far_omega, omega_ref),
+                (far_qt, qt_ref),
+                (far_st, st_ref),
+                (far_inv, inv_ref),
+                (far_fwd, fwd_ref),
+            )
+        )
+    ]
+    for table in tables:
+        table.start()
+    pl.semaphore_wait(barrier, ring - 1)
+
+    def owner(i):
+        return device_of(plane * nf + i, nf, planes)
+
+    def holder(i):
+        return i, part
+
+    def is_me(device):
+        return (device[0] == me) & (device[1] == plane)
+
+    def exchange(k, source, landing, target, origin, pick, mine, size, first):
+        def rows_of(ref, i):
+            return ref.at[pl.ds(pl.multiple_of(i * size, 8), size), :]
+
+        def copy(i):
             return pltpu.make_async_remote_copy(
-                src_ref=src,
-                dst_ref=dst,
-                send_sem=send_sem.at[k, d],
-                recv_sem=recv_sem.at[k, d],
-                device_id={"freq": other, "plane": plane},
+                src_ref=rows_of(source, pick(i)),
+                dst_ref=rows_of(landing, mine),
+                send_sem=send_sem.at[k, i],
+                recv_sem=recv_sem.at[k, mine],
+                device_id=named(target(i)),
                 device_id_type=MESH,
             )
 
-        own = pltpu.make_async_copy(
-            source.at[pl.ds(pl.multiple_of(index_to(me) * size, 8), size), :],
-            landing.at[pl.ds(pl.multiple_of(mine * size, 8), size), :],
-            own_sem.at[k],
-        )
-        if first:
-
-            @pl.loop(1, nf)
-            def _(d):
-                copy(d).start()
-
-            own.start()
-        else:
-
-            @pl.loop(1, nf)
-            def _(d):
-                copy(d).wait()
-
-            own.wait()
-
-    def to_block(f):
-        return block_of(f, plane, nf)
-
-    def to_freq(f):
-        return f
-
-    base_args = (1, s_base, r_base, to_block, me, base_rows)
-    state_args = (0, s_state, r_state, to_block, me, rows)
-    w_args = (2, s_w, r_w, lambda f: 0, block, w_rows)
-    out_state_args = (3, o_state, g_state, to_freq, block, rows)
-    out_forcing_args = (4, o_forcing, g_forcing, to_freq, block, rows)
+        def arrival(i):
+            return pltpu.make_async_remote_copy(
+                src_ref=rows_of(landing, i),
+                dst_ref=rows_of(landing, i),
+                send_sem=send_sem.at[k, i],
+                recv_sem=recv_sem.at[k, i],
+                device_id=named(origin(i)),
+                device_id_type=MESH,
+            )
+
+        def own(i):
+            return pltpu.make_async_copy(
+                rows_of(source, pick(i)), rows_of(landing, mine), own_sem.at[k]
+            )
+
+        @pl.loop(0, nf)
+        def _(d):
+            i = (d + me) % nf
+            stays = is_me(target(i))
+
+            @pl.when(stays)
+            def _():
+                if first:
+                    own(i).start()
+                else:
+                    own(i).wait()
+
+            @pl.when(jnp.logical_not(stays))
+            def _():
+                if first:
+                    copy(i).start()
+                else:
+                    copy(i).wait_send()
+
+            if not first:
+
+                @pl.when(jnp.logical_not(is_me(origin(i))))
+                def _():
+                    arrival(i).wait_recv()
+
+    def same(i):
+        return i
+
+    base_args = (1, s_base, r_base, owner, holder, same, me, base_rows)
+    state_args = (0, s_state, r_state, owner, holder, same, me, rows)
+    w_args = (2, s_w, r_w, holder, owner, lambda i: 0, block, w_rows)
+    out_state_args = (3, o_state, g_state, holder, owner, same, block, rows)
+    out_forcing_args = (4, o_forcing, g_forcing, holder, owner, same, block, rows)
     exchange(*base_args, True)
 
     def halo_copies(e):
@@ -287,6 +336,8 @@
         for copy in edge_copies(e):
             copy.start()
 
+    for table in tables:
+        table.wait()
     load_state.wait()
     send_edges(0, 0)
     load_forcing.wait()
@@ -499,8 +550,8 @@
     inverse, forward = transform_tables(mode_ids, freqs, ntime)
     omegas = np.broadcast_to((0.5 * mode_ids / freqs).astype(np.float32)[:, None], (freqs, radii))
     plane = lax.axis_index("plane")
-    block = block_of(lax.axis_index("freq"), plane, nf)
-    shape_az = chevron(lobe_count, own_az, plane * span_az + block * own_az, span_az * planes)
+    here = ring_of(lax.axis_index("freq"), plane, nf, planes)
+    shape_az = chevron(lobe_count, own_az, here * own_az, span_az * planes)
 
     def padded_rows(count):
         return -(-count // 8) * 8
@@ -521,7 +572,6 @@
     edge_rows = padded_rows(runs)
     first_mode = lax.axis_index("freq") * per_dev
     rates = 0.5 * (first_mode + jnp.arange(per_dev)).astype(jnp.float32) / freqs
-    vmem = pl.BlockSpec(memory_space=pltpu.VMEM)
     smem = pl.BlockSpec(memory_space=pltpu.SMEM)
     anywhere = pl.BlockSpec(memory_space=pl.ANY)
     packed = (nf * rows, radii)
@@ -529,7 +579,7 @@
     outs = pl.pallas_call(
         functools.partial(march, dims),
         out_shape=[jax.ShapeDtypeStruct(packed, f32)] * 2,
-        in_specs=[smem, smem, smem, anywhere, anywhere, anywhere] + [vmem] * 5,
+        in_specs=[smem, smem, smem, anywhere, anywhere, anywhere] + [anywhere] * 5,
         out_specs=[anywhere, anywhere],
         scratch_shapes=[
             pltpu.VMEM(packed, f32),
@@ -556,6 +606,12 @@
             pltpu.SemaphoreType.DMA((2, SWEEPS)),
             pltpu.SemaphoreType.DMA((2, SWEEPS)),
             pltpu.SemaphoreType.DMA((2,)),
+            pltpu.VMEM((freqs, radii), f32),
+            pltpu.VMEM((2 * radii, 2 * radii), jnp.bfloat16),
+            pltpu.VMEM((2 * radii, 2 * radii), jnp.bfloat16),
+            pltpu.VMEM((ntime, 8 * freqs), jnp.bfloat16),
+            pltpu.VMEM((2 * freqs, 4 * ntime), jnp.bfloat16),
+            pltpu.SemaphoreType.DMA((5,)),
         ],
         compiler_params=pltpu.CompilerParams(
             collective_id=0, has_side_effects=True, vmem_limit_bytes=48 * 1024 * 1024

time: 164 us -> 160 us (0.976)
  Pallas kernels: 152 us -> 147 us
    pallas_call x1, Pallas kernels: 152 us -> 147 us  [per_device(): pl.pallas_call(functools.partial(march, dims), out_shape=[jax.ShapeDtypeS...]
where the time goes in v2:
time: 160 us; the launch traced here: 159 us
  Pallas kernels  147 us (92%)
  local copies, waits for them, and re-layouts  10.7 us (7%)
    pallas_call x1, Pallas kernels, per_device(): pl.pallas_call(functools.partial(march, dims), out_shape=[jax.ShapeDtypeS...  147 us
    unnamed x14, local copies, waits for them, and re-layouts  6.59 us

profile of v2, /device:TPU:14, one launch (start us, length us, event | category | flops | bytes accessed | tf_op | source)
XLA Modules:
  0.0 159.2 jit_solution(5728681539964904686)
XLA Ops:
  1.4 0.1 fusion.4.shape_ref
  1.4 1.0 copy.12
  2.4 0.7 jit_solution_.3.far_omega
  3.2 0.0 copy-start
  3.2 1.3 copy-done
  4.5 0.0 copy-start.1
  4.5 1.3 copy-done.1
  5.8 0.0 copy-start.2
  5.8 0.9 copy-done.2
  6.7 0.0 copy-start.3
  6.7 0.9 copy-done.3
  7.6 0.0 copy-start.4
  7.6 0.8 copy-done.4
  8.4 0.0 copy-start.5
  8.4 0.7 copy-done.5
  9.1 0.0 copy-start.6
  9.1 0.7 copy-done.6
  9.8 147.0 %shard_map.113 = (f32[2560,128]{1,0:T(8,128)S(1)}, f32[2560,128]{1,0:T(8,128)S(1)}) custom-call(s32[2]{0:T(128)S(1)} %copy-done.6, f32[8]{0:T(128)S(1)} %fusion.4.shape_ref, f32[2]{0:T(128)S(1)} %convert_multiply_fusion.rate_ref, f32[20,128,128]{2,1,0:T(8,128)S(1)} %bitcast.16, f32[640,128]{1,0:T(8,128)S(1)} %bitcast.18, f32[20,128,128]{2,1,0:T(8,128)S(1)} %bitcast.17, ...), custom_call_target="tpu_custom_call" | custom-call | tf_op jit(solution)/shard_map/pallas_call | solution.py:579
  156.8 1.2 copy.13
  158.0 1.2 copy.14
  (1 shorter events, 0.0 us)
Async XLA Ops:
  3.2 1.3 copy-start
  4.5 1.3 copy-start.1
  5.8 0.9 copy-start.2
  6.7 0.9 copy-start.3
  7.6 0.8 copy-start.4
  8.4 0.7 copy-start.5
  9.1 0.7 copy-start.6

commit v3 on v2

--- a/solution.py
+++ b/solution.py
@@ -614,7 +614,7 @@
             pltpu.SemaphoreType.DMA((5,)),
         ],
         compiler_params=pltpu.CompilerParams(
-            collective_id=0, has_side_effects=True, vmem_limit_bytes=48 * 1024 * 1024
+            collective_id=0, has_side_effects=True, vmem_limit_bytes=63_000 * 1024
         ),
     )(
         station_index,

time: 160 us -> 157 us (0.981)
  local copies, waits for them, and re-layouts: 10.7 us -> 6.87 us
    unnamed x14 -> x2, local copies, waits for them, and re-layouts: 6.59 us -> 0.01 us
where the time goes in v3:
time: 157 us
  Pallas kernels  147 us (94%)
  local copies, waits for them, and re-layouts  6.87 us (4%)
    pallas_call x1, Pallas kernels, per_device(): pl.pallas_call(functools.partial(march, dims), out_shape=[jax.ShapeDtypeS...  147 us
    transpose x2, local copies, waits for them, and re-layouts, finish(): y.transpose(1, 0, 2, 3).reshape(2, per_dev, variables, nf * own_az, radii)  3.82 us

profile of v3, /device:TPU:14, one launch (start us, length us, event | category | flops | bytes accessed | tf_op | source)
XLA Modules:
  0.0 156.6 jit_solution(11956324473388836216)
XLA Ops:
  1.4 0.6 fusion.4.shape_ref
  1.9 0.6 convert_multiply_fusion.rate_ref
  2.5 1.7 %copy.12 = f32[5,16,8,128]{3,2,0,1:T(8,128)} copy(f32[5,16,8,128]{3,2,1,0:T(8,128)} %bitcast.23) | data formatting | bytes 655360 | tf_op jit(solution)/shard_map/reshape | solution.py:560
  4.2 1.3 jit_solution_.3.far_omega
  5.5 147.3 %shard_map.113 = (f32[2560,128]{1,0:T(8,128)}, f32[2560,128]{1,0:T(8,128)}) custom-call(s32[2]{0:T(128)} %station_ref.1, f32[8]{0:T(128)} %fusion.4.shape_ref, f32[2]{0:T(128)} %convert_multiply_fusion.rate_ref, f32[20,128,128]{2,1,0:T(8,128)} %bitcast.16, f32[640,128]{1,0:T(8,128)} %bitcast.18, f32[20,128,128]{2,1,0:T(8,128)} %bitcast.17, ...), custom_call_target="tpu_custom_call" | custom-call | tf_op jit(solution)/shard_map/pallas_call | solution.py:579
  152.8 0.0 copy-start
  152.8 2.6 %copy.13 = f32[20,16,8,128]{3,2,1,0:T(8,128)} copy(f32[20,16,8,128]{3,2,0,1:T(8,128)} %bitcast.20) | data formatting | bytes 2621440 | tf_op jit(solution)/shard_map/transpose | solution.py:638
  155.4 0.0 copy-done
  155.4 1.2 copy.14
Async XLA Ops:
  152.8 2.6 %copy-start = (f32[2560,128]{1,0:T(8,128)S(1)}, f32[2560,128]{1,0:T(8,128)}, u32[]{:S(2)}) copy-start(f32[2560,128]{1,0:T(8,128)} %get-tuple-element.5) | copy-start | bytes 3932164
